TPU v7x, 32 devices: a whole 2x2x4 slice. The times are simulated.
32 devices in a mesh: tm: 8 (over y, x, core), space: 4 (over z).
Axes of the slice: x: 2, y: 2, z: 4, core: 2. Of those that a mesh axis runs over, the one named last changes fastest.
Arguments:
- start_field: float32 [8, 64, 1024], P('tm', None, 'space'), may hold values from -6 to 6
- play_level: int32 [8, 64, 1024], P('tm', None, 'space'), may hold values from -8 to 8
- stiffness: float32 [4, 64, 64, 1024], P(None, None, None, 'space')
- columns: int32 [4, 1024], P(None, 'space'), may hold values from 0 to 287, as said below
- play_width: float32 [64, 1024], P(None, 'space'), may hold values from 0.05 to 0.5
- coil: float32 [3, 64, 1024], P(None, None, 'space'), may hold values from -6 to 6
- newton_counts: int32 [8, 4], P('tm'), may hold values from 1 to 3, as said below
Outputs:
- field_starts: float32 [8, 64, 1024], P('tm', None, 'space')
- play_starts: float32 [8, 64, 1024], P('tm', None, 'space')
Inputs may be any that keep to these rules, and one draw needn't show every extreme that they name: `columns`: slot 0 is the block itself, 16 plus its local index; every slot lies within 16 of that, counting the partition's blocks extended by 16 interface blocks on each side. `newton_counts`: the same for all partitions of a slice.
All inputs are finite; a program needn't handle non-finite values.
Results may differ from a plain program's by a relative error of at most 0.00016.
Values sent between devices are 32-bit elements; how exact they have to be, the bound alone decides.
A program may use at most 64 MiB of HBM per device.

v0:
```python
import functools
import math

import jax
import jax.numpy as jnp
from jax import lax
from jax.experimental import pallas as pl
from jax.experimental.pallas import tpu as pltpu
from jax.sharding import PartitionSpec as P

NIF = 16
NEWT = 3
ITERS = 2
ROWS = 8
LANES = 128

tau_step = 0.5
play_gain = 1.0
play_quantum = 0.05

MESH = pl.DeviceIdType.MESH


def merge_rows(sums):
    row = lax.broadcasted_iota(jnp.int32, (ROWS, LANES), 0)
    width = 1
    while len(sums) > 1:
        low = (row & width) == 0
        sums = [
            jnp.where(low, even, odd) + pltpu.roll(jnp.where(low, odd, even), width, 0)
            for even, odd in zip(sums[::2], sums[1::2])
        ]
        width *= 2
    return sums[0]


def play(state, guess, width):
    return jnp.minimum(jnp.maximum(state, guess - width), guess + width)


def kernel(
    slices, parts, strides,
    start_ref, level_ref, stiff_hbm, columns_ref, width_ref, coil_ref, counts_ref,
    out_ref,
    stiff, guess, field, state, damp, first, picked, source, index, inside,
    edge_out, edge_in, own, mixed, arrived,
    stiff_sem, edge_send, edge_recv, scan_send, scan_recv,
):
    nnz, blk, _, local = stiff.shape
    groups, tiles = blk // ROWS, local // LANES
    steps = counts_ref.shape[1]
    slice_index = lax.axis_index("tm")
    part = lax.axis_index("space")
    has_left, has_right = part > 0, part < parts - 1

    loads = [
        pltpu.make_async_copy(stiff_hbm.at[s], stiff.at[s], stiff_sem.at[s]) for s in range(nnz)
    ]
    for load in loads:
        load.start()

    edge_in[...] = jnp.zeros_like(edge_in)
    offsets = sorted({d % slices for d in strides} | {-d % slices for d in strides})
    barrier = pltpu.get_barrier_semaphore()
    for offset in offsets:
        pl.semaphore_signal(
            barrier, inc=1, device_id={"tm": lax.rem(slice_index + offset, slices)},
            device_id_type=MESH,
        )

    @pl.when(has_left)
    def _():
        pl.semaphore_signal(barrier, inc=1, device_id={"space": part - 1}, device_id_type=MESH)

    @pl.when(has_right)
    def _():
        pl.semaphore_signal(barrier, inc=1, device_id={"space": part + 1}, device_id_type=MESH)

    lane = lax.broadcasted_iota(jnp.int32, (ROWS, LANES), 1)
    row = lax.broadcasted_iota(jnp.int32, (ROWS, LANES), 0)
    group_of_lane = lane // NIF

    def rows(g):
        return pl.ds(g * ROWS if isinstance(g, int) else pl.multiple_of(g * ROWS, ROWS), ROWS)

    def tile(t):
        return pl.ds(t * LANES, LANES)

    for s in range(1, nnz):
        for t in range(tiles):
            place = columns_ref[s : s + 1, t * LANES : (t + 1) * LANES] - (NIF + t * LANES)
            place = jnp.broadcast_to(place, (ROWS, LANES))
            index[s - 1, t] = place & (LANES - 1)
            inside[s - 1, t] = jnp.where((place >= 0) & (place < LANES), 1, 0)

    for step in range(steps):
        moment = (slice_index.astype(jnp.float32) * steps + (step + 1)) * (
            2.0 * math.pi / (slices * steps)
        )
        waves = [
            jnp.sin(jnp.full((ROWS, LANES), moment + h * (2.0 * math.pi / 3.0), jnp.float32))
            for h in range(3)
        ]
        for g in range(groups):
            for t in range(tiles):
                here = (rows(g), tile(t))
                source[(step, *here)] = (
                    waves[0] * coil_ref[(0, *here)]
                    + waves[1] * coil_ref[(1, *here)]
                    + waves[2] * coil_ref[(2, *here)]
                )

    field[...] = start_ref[0]
    guess[...] = start_ref[0]
    state[0] = level_ref[0].astype(jnp.float32) * play_quantum
    state[1] = level_ref[0].astype(jnp.float32) * play_quantum

    loads[0].wait()
    for g in range(groups):
        for t in range(tiles):
            diag = jnp.zeros((ROWS, LANES), jnp.float32)
            for r in range(ROWS):
                diag = jnp.where(row == r, stiff[0, g * ROWS + r, rows(g), tile(t)], diag)
            damp[rows(g), tile(t)] = 1.0 / (1.0 + tau_step * (diag + play_gain))

    pl.semaphore_wait(
        barrier, len(offsets) + has_left.astype(jnp.int32) + has_right.astype(jnp.int32)
    )

    def products(slots, g, t):
        sums = [None] * ROWS
        for s in slots:
            for b in range(groups):
                vector = guess[rows(b), tile(t)] if s == 0 else picked[s - 1, rows(b), tile(t)]
                for r in range(ROWS):
                    term = stiff[s, g * ROWS + r, rows(b), tile(t)] * vector
                    sums[r] = term if sums[r] is None else sums[r] + term
        return merge_rows(sums)

    def sweep(step, counter, begin):
        slot = lax.rem(step * NEWT + counter, 2)
        upper = lower = None
        for b in range(groups):
            last = guess[rows(b), tile(tiles - 1)]
            head = guess[rows(b), tile(0)]
            if b == 0:
                upper, lower = last, head
            else:
                upper = jnp.where(
                    group_of_lane == LANES // NIF - 1 - b,
                    pltpu.roll(last, LANES - NIF * b, 1), upper,
                )
                lower = jnp.where(group_of_lane == b, pltpu.roll(head, NIF * b, 1), lower)
        edge_out[0] = upper
        edge_out[1] = lower
        up = pltpu.make_async_remote_copy(
            src_ref=edge_out.at[0], dst_ref=edge_in.at[0, slot],
            send_sem=edge_send.at[0], recv_sem=edge_recv.at[0, slot],
            device_id={"space": part + 1}, device_id_type=MESH,
        )
        down = pltpu.make_async_remote_copy(
            src_ref=edge_out.at[1], dst_ref=edge_in.at[1, slot],
            send_sem=edge_send.at[1], recv_sem=edge_recv.at[1, slot],
            device_id={"space": part - 1}, device_id_type=MESH,
        )

        @pl.when(has_right)
        def _():
            up.start()

        @pl.when(has_left)
        def _():
            down.start()

        @pl.loop(0, groups)
        def _(g):
            for t in range(tiles):
                first[rows(g), tile(t)] = products((0,), g, t)

        begin(counter)

        @pl.when(has_right)
        def _():
            up.wait_send()
            down.wait_recv()

        @pl.when(has_left)
        def _():
            down.wait_send()
            up.wait_recv()

        left_edge, right_edge = edge_in[0, slot], edge_in[1, slot]
        for b in range(groups):
            blocks = [guess[rows(b), tile(t)] for t in range(tiles)]
            before = left_edge if b == 0 else pltpu.roll(left_edge, NIF * b, 1)
            after = right_edge if b == 0 else pltpu.roll(right_edge, LANES - NIF * b, 1)
            chain = [before, *blocks, after]
            for t in range(tiles):
                beside = jnp.where(lane < LANES // 2, chain[t + 2], chain[t])
                for s in range(1, nnz):
                    where = index[s - 1, t]
                    picked[s - 1, rows(b), tile(t)] = jnp.where(
                        inside[s - 1, t] == 1,
                        jnp.take_along_axis(blocks[t], where, axis=1, mode="promise_in_bounds"),
                        jnp.take_along_axis(beside, where, axis=1, mode="promise_in_bounds"),
                    )

        active = jnp.full((ROWS, LANES), counter, jnp.int32) < jnp.full(
            (ROWS, LANES), counts_ref[0, step], jnp.int32
        )

        @pl.loop(0, groups)
        def _(g):
            for t in range(tiles):
                here = (rows(g), tile(t))
                applied = first[here] + products(range(1, nnz), g, t)
                x = guess[here]
                bound = play(state[(0, *here)], x, width_ref[here])
                resid = x - field[here] - tau_step * (
                    source[(step, *here)] - applied - play_gain * bound
                )
                guess[here] = jnp.where(active, x - resid * damp[here], x)

    def wait_stiffness(counter):
        @pl.when(counter == 0)
        def _():
            for load in loads[1:]:
                load.wait()

    for round_ in range(ITERS):

        @pl.loop(0, steps)
        def _(step):
            @pl.loop(0, NEWT)
            def _(counter):
                if round_ == 0:
                    sweep(step, counter, lambda c: wait_stiffness(step * NEWT + c))
                else:
                    sweep(step, counter, lambda c: None)

            state[0] = play(state[0], guess[...], width_ref[...])
            field[...] = guess[...]

        begin_a = start_ref[0] if round_ == 0 else out_ref[0, 0]
        fine_a, fine_p = guess[...], state[0]
        full = jnp.full((blk, local), slice_index, jnp.int32) == slices - 1
        own[round_, 0] = jnp.where(full, fine_a, fine_a - damp[...] * begin_a)
        own[round_, 1] = jnp.where(full, fine_p, fine_p - state[1])

        def send(source_ref, place, distance):
            return pltpu.make_async_remote_copy(
                src_ref=source_ref, dst_ref=arrived.at[round_, place],
                send_sem=scan_send.at[round_, place], recv_sem=scan_recv.at[round_, place],
                device_id={"tm": lax.rem(slice_index + distance, slices)},
                device_id_type=MESH,
            )

        near = send(own.at[round_], 0, 1)
        near.start()
        far = send(own.at[round_], 1, 2)

        @pl.when(slice_index != slices - 2)
        def _():
            far.start()

        near.wait_recv()
        mixed[round_, 0] = arrived[round_, 0]

        @pl.when(slice_index != 0)
        def _():
            far.wait_recv()
            mixed[round_, 0, 0] = arrived[round_, 0, 0] + damp[...] * arrived[round_, 1, 0]
            mixed[round_, 0, 1] = arrived[round_, 0, 1] + arrived[round_, 1, 1]

        near.wait_send()

        @pl.when(slice_index != slices - 2)
        def _():
            far.wait_send()

        power = damp[...]
        stage, distance = 0, 2
        while distance < slices:
            power = power * power
            hop = send(mixed.at[round_, stage], stage + 2, distance)

            @pl.when(slice_index + distance < slices)
            def _():
                hop.start()

            mixed[round_, stage + 1] = mixed[round_, stage]

            @pl.when(slice_index >= distance)
            def _():
                hop.wait_recv()
                mixed[round_, stage + 1, 0] = (
                    mixed[round_, stage, 0] + power * arrived[round_, stage + 2, 0]
                )
                mixed[round_, stage + 1, 1] = (
                    mixed[round_, stage, 1] + arrived[round_, stage + 2, 1]
                )

            @pl.when(slice_index + distance < slices)
            def _():
                hop.wait_send()

            stage, distance = stage + 1, distance * 2

        out_ref[0, 0] = mixed[round_, stage, 0]
        out_ref[1, 0] = mixed[round_, stage, 1]
        if round_ < ITERS - 1:
            guess[...] = mixed[round_, stage, 0]
            field[...] = mixed[round_, stage, 0]
            state[0] = mixed[round_, stage, 1]
            state[1] = mixed[round_, stage, 1]


def on_device(start_field, play_level, stiffness, columns, play_width, coil, newton_counts):
    slices, parts = lax.axis_size("tm"), lax.axis_size("space")
    nnz, blk, _, local = stiffness.shape
    strides = [1, 2]
    while strides[-1] * 2 < slices:
        strides.append(strides[-1] * 2)
    stages = len(strides) - 1
    tiles, groups, steps = local // LANES, blk // ROWS, newton_counts.shape[1]
    vmem = pl.BlockSpec(memory_space=pltpu.VMEM)
    plane = (blk, local)
    f32 = jnp.float32
    both = pl.pallas_call(
        functools.partial(kernel, slices, parts, strides),
        out_shape=jax.ShapeDtypeStruct((2, 1, *plane), f32),
        in_specs=[
            vmem, vmem, pl.BlockSpec(memory_space=pl.ANY), vmem, vmem, vmem,
            pl.BlockSpec(memory_space=pltpu.SMEM),
        ],
        out_specs=vmem,
        scratch_shapes=[
            pltpu.VMEM(stiffness.shape, f32),
            pltpu.VMEM(plane, f32),
            pltpu.VMEM(plane, f32),
            pltpu.VMEM((2, *plane), f32),
            pltpu.VMEM(plane, f32),
            pltpu.VMEM(plane, f32),
            pltpu.VMEM((nnz - 1, *plane), f32),
            pltpu.VMEM((steps, *plane), f32),
            pltpu.VMEM((nnz - 1, tiles, ROWS, LANES), jnp.int32),
            pltpu.VMEM((nnz - 1, tiles, ROWS, LANES), jnp.int32),
            pltpu.VMEM((2, ROWS, LANES), f32),
            pltpu.VMEM((2, 2, ROWS, LANES), f32),
            pltpu.VMEM((ITERS, 2, *plane), f32),
            pltpu.VMEM((ITERS, stages + 1, 2, *plane), f32),
            pltpu.VMEM((ITERS, stages + 2, 2, *plane), f32),
            pltpu.SemaphoreType.DMA((nnz,)),
            pltpu.SemaphoreType.DMA((2,)),
            pltpu.SemaphoreType.DMA((2, 2)),
            pltpu.SemaphoreType.DMA((ITERS, stages + 2)),
            pltpu.SemaphoreType.DMA((ITERS, stages + 2)),
        ],
        compiler_params=pltpu.CompilerParams(
            collective_id=0, has_side_effects=True, vmem_limit_bytes=48 * 1024 * 1024
        ),
        name="parareal",
    )(start_field, play_level, stiffness, columns, play_width, coil, newton_counts)
    return both[0], both[1]


def solution(mesh):
    return jax.shard_map(
        on_device,
        mesh=mesh,
        in_specs=(
            P("tm", None, "space"),
            P("tm", None, "space"),
            P(None, None, None, "space"),
            P(None, "space"),
            P(None, "space"),
            P(None, None, "space"),
            P("tm", None),
        ),
        out_specs=(P("tm", None, "space"), P("tm", None, "space")),
        check_vma=False,
    )
```

profile of v0, /device:TPU:0, one launch (start us, length us, event | category | flops | bytes accessed | tf_op | source)
XLA Modules:
  0.0 133.2 jit_solution(11764439369466341150)
XLA Ops:
  0.6 0.0 copy-start
  0.6 0.9 copy-done
  1.6 0.0 copy-start.1
  1.6 0.8 copy-done.1
  2.4 0.0 copy-start.2
  2.4 0.8 copy-done.2
  3.2 0.0 copy-start.3
  3.2 0.8 copy-done.3
  4.1 0.0 copy-start.4
  4.1 0.7 copy-done.4
  4.8 0.0 copy-start.5
  4.8 0.7 copy-done.5
  5.4 127.1 %parareal.1 = f32[2,1,64,256]{3,2,1,0:T(8,128)S(1)} custom-call(f32[1,64,256]{2,1,0:T(8,128)S(1)} %copy-done.1, s32[1,64,256]{2,1,0:T(8,128)S(1)} %copy-done.2, f32[4,64,64,256]{3,2,1,0:T(8,128)} %stiff_hbm.1, s32[4,256]{1,0:T(4,128)S(1)} %copy-done.4, f32[64,256]{1,0:T(8,128)S(1)} %copy-done.3, f32[3,64,256]{2,1,0:T(8,128)S(1)} %copy-done, s32[1,4]{1,0:T(1,128)S(1)} %copy-done.5), custom_call_target="tpu_custom_call" | custom-call | tf_op jit(solution)/shard_map/parareal/pallas_call | solution.py:329
  132.6 0.7 slice_bitcast_fusion
Async XLA Ops:
  0.6 0.9 copy-start
  1.6 0.8 copy-start.1
  2.4 0.8 copy-start.2
  3.2 0.8 copy-start.3
  4.1 0.7 copy-start.4
  4.8 0.7 copy-start.5
where the time goes:
time: 134 us; the launch traced here: 133 us
  Pallas kernels  127 us (95%)
  local copies, waits for them, and re-layouts  5.44 us (4%)
    pallas_call x1, Pallas kernels, on_device(): pl.pallas_call(functools.partial(kernel, slices, parts, strides), out_sha...  127 us
    unnamed x12, local copies, waits for them, and re-layouts  4.78 us

commit v1 on v0

--- a/solution.py
+++ b/solution.py
@@ -40,9 +40,11 @@
 
 def kernel(
     slices, parts, strides,
-    start_ref, level_ref, stiff_hbm, columns_ref, width_ref, coil_ref, counts_ref,
+    start_hbm, level_hbm, stiff_hbm, columns_hbm, width_hbm, coil_hbm, counts_ref,
     out_ref,
+    start_ref, level_ref, columns_ref, width_ref, coil_ref, small_sem,
     stiff, guess, field, state, damp, first, picked, source, index, inside,
+    edge_stiff, edge_picked, edge_index, edge_valid,
     edge_out, edge_in, own, mixed, arrived,
     stiff_sem, edge_send, edge_recv, scan_send, scan_recv,
 ):
@@ -53,6 +55,15 @@
     part = lax.axis_index("space")
     has_left, has_right = part > 0, part < parts - 1
 
+    small = [
+        pltpu.make_async_copy(source_, target, small_sem.at[k])
+        for k, (source_, target) in enumerate((
+            (columns_hbm, columns_ref), (coil_hbm, coil_ref), (start_hbm, start_ref),
+            (level_hbm, level_ref), (width_hbm, width_ref),
+        ))
+    ]
+    for load in small:
+        load.start()
     loads = [
         pltpu.make_async_copy(stiff_hbm.at[s], stiff.at[s], stiff_sem.at[s]) for s in range(nnz)
     ]
@@ -80,18 +91,31 @@
     row = lax.broadcasted_iota(jnp.int32, (ROWS, LANES), 0)
     group_of_lane = lane // NIF
 
+    def take(values, where):
+        return jnp.take_along_axis(values, where, axis=1, mode="promise_in_bounds")
+
     def rows(g):
         return pl.ds(g * ROWS if isinstance(g, int) else pl.multiple_of(g * ROWS, ROWS), ROWS)
 
     def tile(t):
         return pl.ds(t * LANES, LANES)
 
+    for load in small:
+        load.wait()
     for s in range(1, nnz):
         for t in range(tiles):
             place = columns_ref[s : s + 1, t * LANES : (t + 1) * LANES] - (NIF + t * LANES)
             place = jnp.broadcast_to(place, (ROWS, LANES))
             index[s - 1, t] = place & (LANES - 1)
             inside[s - 1, t] = jnp.where((place >= 0) & (place < LANES), 1, 0)
+            if t == 0:
+                near = take(place, lane & (NIF - 1))
+                edge_index[0, s - 1] = group_of_lane * NIF + (near & (NIF - 1))
+                edge_valid[0, s - 1] = jnp.where(near < 0, 1.0, 0.0)
+            if t == tiles - 1:
+                near = take(place, LANES - NIF + (lane & (NIF - 1)))
+                edge_index[1, s - 1] = group_of_lane * NIF + (near & (NIF - 1))
+                edge_valid[1, s - 1] = jnp.where(near >= LANES, 1.0, 0.0)
 
     for step in range(steps):
         moment = (slice_index.astype(jnp.float32) * steps + (step + 1)) * (
@@ -127,6 +151,24 @@
         barrier, len(offsets) + has_left.astype(jnp.int32) + has_right.astype(jnp.int32)
     )
 
+    for s in range(1, nnz):
+        loads[s].wait()
+
+        @pl.loop(0, blk, unroll=8)
+        def _(a):
+            left = right = None
+            for b in range(groups):
+                head = stiff[s, a, rows(b), tile(0)]
+                last = stiff[s, a, rows(b), tile(tiles - 1)]
+                q = LANES // NIF - 1 - b
+                head = head if q == 0 else pltpu.roll(head, NIF * q, 1)
+                shift = (NIF * b + NIF) % LANES
+                last = last if shift == 0 else pltpu.roll(last, shift, 1)
+                left = head if b == 0 else jnp.where(group_of_lane == q, head, left)
+                right = last if b == 0 else jnp.where(group_of_lane == b, last, right)
+            edge_stiff[0, s - 1, a] = jnp.where(edge_valid[0, s - 1] == 1.0, left, 0.0)
+            edge_stiff[1, s - 1, a] = jnp.where(edge_valid[1, s - 1] == 1.0, right, 0.0)
+
     def products(slots, g, t):
         sums = [None] * ROWS
         for s in slots:
@@ -137,7 +179,7 @@
                     sums[r] = term if sums[r] is None else sums[r] + term
         return merge_rows(sums)
 
-    def sweep(step, counter, begin):
+    def sweep(step, counter):
         slot = lax.rem(step * NEWT + counter, 2)
         upper = lower = None
         for b in range(groups):
@@ -172,48 +214,65 @@
         def _():
             down.start()
 
-        @pl.loop(0, groups)
-        def _(g):
-            for t in range(tiles):
-                first[rows(g), tile(t)] = products((0,), g, t)
-
-        begin(counter)
-
-        @pl.when(has_right)
-        def _():
-            up.wait_send()
-            down.wait_recv()
-
-        @pl.when(has_left)
-        def _():
-            down.wait_send()
-            up.wait_recv()
-
-        left_edge, right_edge = edge_in[0, slot], edge_in[1, slot]
+        nothing = jnp.zeros((ROWS, LANES), jnp.float32)
         for b in range(groups):
             blocks = [guess[rows(b), tile(t)] for t in range(tiles)]
-            before = left_edge if b == 0 else pltpu.roll(left_edge, NIF * b, 1)
-            after = right_edge if b == 0 else pltpu.roll(right_edge, LANES - NIF * b, 1)
-            chain = [before, *blocks, after]
+            chain = [nothing, *blocks, nothing]
             for t in range(tiles):
                 beside = jnp.where(lane < LANES // 2, chain[t + 2], chain[t])
                 for s in range(1, nnz):
                     where = index[s - 1, t]
                     picked[s - 1, rows(b), tile(t)] = jnp.where(
-                        inside[s - 1, t] == 1,
-                        jnp.take_along_axis(blocks[t], where, axis=1, mode="promise_in_bounds"),
-                        jnp.take_along_axis(beside, where, axis=1, mode="promise_in_bounds"),
+                        inside[s - 1, t] == 1, take(blocks[t], where), take(beside, where)
                     )
+
+        @pl.loop(0, groups)
+        def _(g):
+            for t in range(tiles):
+                first[rows(g), tile(t)] = products(range(nnz), g, t)
+
+        @pl.when(has_right)
+        def _():
+            up.wait_send()
+            down.wait_recv()
+
+        @pl.when(has_left)
+        def _():
+            down.wait_send()
+            up.wait_recv()
+
+        for side in range(2):
+            edge = edge_in[side, slot]
+            for s in range(1, nnz):
+                edge_picked[side, s - 1] = take(edge, edge_index[side, s - 1])
 
         active = jnp.full((ROWS, LANES), counter, jnp.int32) < jnp.full(
             (ROWS, LANES), counts_ref[0, step], jnp.int32
         )
 
-        @pl.loop(0, groups)
-        def _(g):
+        def edge_products(side, g):
+            total = merge_rows([
+                sum(
+                    edge_stiff[side, s, g * ROWS + r] * edge_picked[side, s]
+                    for s in range(nnz - 1)
+                )
+                for r in range(ROWS)
+            ])
+            width = LANES // 2
+            while width >= NIF:
+                total = total + pltpu.roll(total, width, 1)
+                width //= 2
+            at_edge = lane < NIF if side == 0 else lane >= LANES - NIF
+            return jnp.where(at_edge, total, 0.0)
+
+        for g in range(groups):
             for t in range(tiles):
                 here = (rows(g), tile(t))
-                applied = first[here] + products(range(1, nnz), g, t)
+                applied = first[here]
+                if t == 0:
+                    applied = applied + edge_products(0, g)
+                if t == tiles - 1:
+                    applied = applied + edge_products(1, g)
                 x = guess[here]
                 bound = play(state[(0, *here)], x, width_ref[here])
                 resid = x - field[here] - tau_step * (
@@ -221,22 +280,13 @@
                 )
                 guess[here] = jnp.where(active, x - resid * damp[here], x)
 
-    def wait_stiffness(counter):
-        @pl.when(counter == 0)
-        def _():
-            for load in loads[1:]:
-                load.wait()
-
     for round_ in range(ITERS):
 
         @pl.loop(0, steps)
         def _(step):
             @pl.loop(0, NEWT)
             def _(counter):
-                if round_ == 0:
-                    sweep(step, counter, lambda c: wait_stiffness(step * NEWT + c))
-                else:
-                    sweep(step, counter, lambda c: None)
+                sweep(step, counter)
 
             state[0] = play(state[0], guess[...], width_ref[...])
             field[...] = guess[...]
@@ -330,11 +380,17 @@
         functools.partial(kernel, slices, parts, strides),
         out_shape=jax.ShapeDtypeStruct((2, 1, *plane), f32),
         in_specs=[
-            vmem, vmem, pl.BlockSpec(memory_space=pl.ANY), vmem, vmem, vmem,
+            *[pl.BlockSpec(memory_space=pltpu.HBM)] * 6,
             pl.BlockSpec(memory_space=pltpu.SMEM),
         ],
         out_specs=vmem,
         scratch_shapes=[
+            pltpu.VMEM(start_field.shape, f32),
+            pltpu.VMEM(play_level.shape, jnp.int32),
+            pltpu.VMEM(columns.shape, jnp.int32),
+            pltpu.VMEM(plane, f32),
+            pltpu.VMEM(coil.shape, f32),
+            pltpu.SemaphoreType.DMA((5,)),
             pltpu.VMEM(stiffness.shape, f32),
             pltpu.VMEM(plane, f32),
             pltpu.VMEM(plane, f32),
@@ -345,6 +401,10 @@
             pltpu.VMEM((steps, *plane), f32),
             pltpu.VMEM((nnz - 1, tiles, ROWS, LANES), jnp.int32),
             pltpu.VMEM((nnz - 1, tiles, ROWS, LANES), jnp.int32),
+            pltpu.VMEM((2, nnz - 1, blk, ROWS, LANES), f32),
+            pltpu.VMEM((2, nnz - 1, ROWS, LANES), f32),
+            pltpu.VMEM((2, nnz - 1, ROWS, LANES), jnp.int32),
+            pltpu.VMEM((2, nnz - 1, ROWS, LANES), f32),
             pltpu.VMEM((2, ROWS, LANES), f32),
             pltpu.VMEM((2, 2, ROWS, LANES), f32),
             pltpu.VMEM((ITERS, 2, *plane), f32),

time: 134 us -> 112 us (0.84)
  Pallas kernels: 127 us -> 105 us
    pallas_call x1, Pallas kernels: 127 us -> 105 us  [on_device(): pl.pallas_call(functools.partial(kernel, slices, parts, strides), out_sha...]
where the time goes in v1:
time: 112 us; the launch traced here: 111 us
  Pallas kernels  105 us (94%)
  local copies, waits for them, and re-layouts  5.44 us (5%)
    pallas_call x1, Pallas kernels, on_device(): pl.pallas_call(functools.partial(kernel, slices, parts, strides), out_sha...  105 us
    unnamed x12, local copies, waits for them, and re-layouts  4.78 us

profile of v1, /device:TPU:0, one launch (start us, length us, event | category | flops | bytes accessed | tf_op | source)
XLA Modules:
  0.0 111.2 jit_solution(14696650073891338372)
XLA Ops:
  0.6 0.0 copy-start
  0.6 0.9 copy-done
  1.6 0.0 copy-start.1
  1.6 0.8 copy-done.1
  2.4 0.0 copy-start.2
  2.4 0.8 copy-done.2
  3.2 0.0 copy-start.3
  3.2 0.8 copy-done.3
  4.1 0.0 copy-start.4
  4.1 0.7 copy-done.4
  4.8 0.0 copy-start.5
  4.8 0.7 copy-done.5
  5.4 105.1 %parareal.1 = f32[2,1,64,256]{3,2,1,0:T(8,128)S(1)} custom-call(f32[1,64,256]{2,1,0:T(8,128)S(1)} %copy-done.1, s32[1,64,256]{2,1,0:T(8,128)S(1)} %copy-done.2, f32[4,64,64,256]{3,2,1,0:T(8,128)} %stiff_hbm.1, s32[4,256]{1,0:T(4,128)S(1)} %copy-done.4, f32[64,256]{1,0:T(8,128)S(1)} %copy-done.3, f32[3,64,256]{2,1,0:T(8,128)S(1)} %copy-done, s32[1,4]{1,0:T(1,128)S(1)} %copy-done.5), custom_call_target="tpu_custom_call" | custom-call | tf_op jit(solution)/shard_map/parareal/pallas_call | solution.py:379
  110.6 0.7 slice_bitcast_fusion
Async XLA Ops:
  0.6 0.9 copy-start
  1.6 0.8 copy-start.1
  2.4 0.8 copy-start.2
  3.2 0.8 copy-start.3
  4.1 0.7 copy-start.4
  4.8 0.7 copy-start.5
